TPU v7x, 32 devices: a whole 2x2x4 slice. The times are simulated.
32 devices in a mesh: rep: 8 (over z, y), ep: 4 (over x, core).
Axes of the slice: x: 2, y: 2, z: 4, core: 2. Of those that a mesh axis runs over, the one named last changes fastest.
Arguments:
- tokens: bfloat16 [16384, 1536], P(('rep', 'ep')), may hold values from -6 to 6
- norm_attn: bfloat16 [1536], replicated, may hold values from 0.099609375 to 1.8984375
- w_query: bfloat16 [1536, 1536], replicated, may hold values from -0.15625 to 0.15625
- key_projection: bfloat16 [1536, 512], replicated, may hold values from -0.15625 to 0.15625
- value_projection: bfloat16 [1536, 512], replicated, may hold values from -0.15625 to 0.15625
- w_out: bfloat16 [1536, 1536], replicated, may hold values from -2.5 to 2.5
- norm_ffn: bfloat16 [1536], replicated, may hold values from 0.099609375 to 1.8984375
- w_router: bfloat16 [1536, 20], replicated, may hold values from -0.078125 to 0.078125
- w_gate: bfloat16 [20, 1536, 512], P('ep'), may hold values from -0.15625 to 0.15625
- w_up: bfloat16 [20, 1536, 512], P('ep'), may hold values from -0.15625 to 0.15625
- w_down: bfloat16 [20, 512, 1536], P('ep'), may hold values from -3 to 3
- routes: int32 [16384, 8], P(('rep', 'ep')), may hold values from 0 to 19, as said below
- cotangent: bfloat16 [16384, 1536], P(('rep', 'ep')), may hold values from -6 to 6
Outputs:
- mixed: bfloat16 [16384, 1536], P(('rep', 'ep'))
- d_input: float32 [16384, 1536], P(('rep', 'ep'))
- grad_norm_attn: float32 [1536], P('ep')
- grad_query: float32 [1536, 1536], P('ep')
- grad_key: float32 [1536, 512], P('ep')
- grad_value: float32 [1536, 512], P('ep')
- grad_out: float32 [1536, 1536], P('ep')
- grad_norm_ffn: float32 [1536], P('ep')
- grad_router: float32 [1536, 20], P('ep')
- grad_gate: float32 [20, 1536, 512], P('ep')
- grad_up: float32 [20, 1536, 512], P('ep')
- grad_down: float32 [20, 512, 1536], P('ep')
Inputs may be any that keep to these rules, and one draw needn't show every extreme that they name: `routes`: each row names 8 different experts. In each aligned block of 512 rows (the rows of one device) no expert is named by more than 384 rows, and in each group of 4 consecutive such blocks one expert is named by exactly 384 rows of every block of the group.
All inputs are finite; a program needn't handle non-finite values.
Results may differ from a plain program's by a relative error of at most 0.02.
Values may be sent and summed in bfloat16 or wider, within the bound.
A program may use at most 448 MiB of HBM per device.

v0:
```python
import math
import jax
import jax.numpy as jnp
from jax import lax
from jax.sharding import PartitionSpec as P

QUERY_HEADS = 24
KEY_VALUE_HEADS = 8
HEAD_SIZE = 64
TOPK = 8
SEQUENCE_TOKENS = 512
BLOCK = 256
epsilon = 1e-06
masked_value = -1e30


def rope_tables(token_count, width):
    half_width = width // 2
    places = (jnp.arange(token_count) % SEQUENCE_TOKENS).astype(jnp.float32)
    rates = jnp.exp(jnp.arange(half_width, dtype=jnp.float32) * (-2.0 * math.log(10000.0) / width))
    angles = places[:, None] * rates[None, :]
    return (jnp.cos(angles)[:, None, :], jnp.sin(angles)[:, None, :])


def apply_rotary(field, cosine_table, sine_table):
    half_width = field.shape[-1] // 2
    first = field[..., :half_width]
    second = field[..., half_width:]
    return jnp.concatenate(
        [first * cosine_table - second * sine_table, second * cosine_table + first * sine_table], -1
    )


def invert_rotary(field, cosine_table, sine_table):
    half_width = field.shape[-1] // 2
    first = field[..., :half_width]
    second = field[..., half_width:]
    return jnp.concatenate(
        [first * cosine_table + second * sine_table, second * cosine_table - first * sine_table], -1
    )


def norm_forward(field, gain):
    inverse = lax.rsqrt(jnp.mean(field * field, -1, keepdims=True) + epsilon)
    normal = field * inverse
    return ((normal * gain.astype(jnp.float32)).astype(jnp.bfloat16), normal, inverse)


def norm_backward(d_normed, normal, inverse, gain):
    scaled = d_normed * gain.astype(jnp.float32)
    d_field = inverse * (scaled - normal * jnp.mean(scaled * normal, -1, keepdims=True))
    return (d_field, jnp.sum(d_normed * normal, 0))


def score_block(queries, key_rows):
    places = jnp.arange(SEQUENCE_TOKENS) // BLOCK
    allowed = places[None, :] <= places[:, None]
    scores = jnp.einsum(
        "qhgd,khd->hgqk", queries, key_rows, preferred_element_type=jnp.float32
    ) * HEAD_SIZE ** (-0.5)
    return jnp.where(allowed, scores, masked_value)


def attend(pack):
    queries, key_rows, value_rows = pack
    scores = score_block(queries, key_rows)
    highest = jnp.max(scores, -1, keepdims=True)
    shifted = jnp.exp(scores - highest)
    totals = jnp.sum(shifted, -1, keepdims=True)
    probs_bf = (shifted / totals).astype(jnp.bfloat16)
    head_mix = jnp.einsum(
        "hgqk,khd->qhgd", probs_bf, value_rows, preferred_element_type=jnp.float32
    )
    return (head_mix.astype(jnp.bfloat16), highest + jnp.log(totals))


def attend_back(pack):
    queries, key_rows, value_rows, d_mix, log_totals = pack
    factor = HEAD_SIZE ** (-0.5)
    scores = score_block(queries, key_rows)
    probs_f = jnp.exp(scores - log_totals)
    probs_bf = probs_f.astype(jnp.bfloat16)
    d_probs = jnp.einsum("qhgd,khd->hgqk", d_mix, value_rows, preferred_element_type=jnp.float32)
    centre = jnp.sum(probs_f * d_probs, -1, keepdims=True)
    d_scores = (probs_f * (d_probs - centre)).astype(jnp.bfloat16)
    d_queries = (
        jnp.einsum("hgqk,khd->qhgd", d_scores, key_rows, preferred_element_type=jnp.float32)
        * factor
    )
    d_keys = (
        jnp.einsum("hgqk,qhgd->khd", d_scores, queries, preferred_element_type=jnp.float32) * factor
    )
    d_values = jnp.einsum("hgqk,qhgd->khd", probs_bf, d_mix, preferred_element_type=jnp.float32)
    return (d_queries, d_keys, d_values)


def per_device(
    tokens,
    norm_attn,
    w_query,
    key_projection,
    value_projection,
    w_out,
    norm_ffn,
    w_router,
    w_gate,
    w_up,
    w_down,
    routes,
    cotangent,
):
    token_count = tokens.shape[0]
    width = tokens.shape[1]
    experts_all = w_router.shape[1]
    query_groups = QUERY_HEADS // KEY_VALUE_HEADS
    sequence_total = token_count // SEQUENCE_TOKENS
    x_float = tokens.astype(jnp.float32)
    cot_all = lax.all_gather(cotangent, "ep", axis=0, tiled=True)
    hidden_first, normal_one, inverse_one = norm_forward(x_float, norm_attn)
    query_unrotated = jnp.dot(hidden_first, w_query, preferred_element_type=jnp.float32)
    key_unrotated = jnp.dot(hidden_first, key_projection, preferred_element_type=jnp.float32)
    value_row_block = jnp.dot(
        hidden_first, value_projection, preferred_element_type=jnp.float32
    ).astype(jnp.bfloat16)
    cosine_table, sine_table = rope_tables(token_count, HEAD_SIZE)
    query_rotated = apply_rotary(
        query_unrotated.reshape(token_count, QUERY_HEADS, HEAD_SIZE), cosine_table, sine_table
    ).astype(jnp.bfloat16)
    key_rotated = apply_rotary(
        key_unrotated.reshape(token_count, KEY_VALUE_HEADS, HEAD_SIZE), cosine_table, sine_table
    ).astype(jnp.bfloat16)
    query_sequence = query_rotated.reshape(
        sequence_total, SEQUENCE_TOKENS, KEY_VALUE_HEADS, query_groups, HEAD_SIZE
    )
    key_sequence = key_rotated.reshape(sequence_total, SEQUENCE_TOKENS, KEY_VALUE_HEADS, HEAD_SIZE)
    value_sequence = value_row_block.reshape(
        sequence_total, SEQUENCE_TOKENS, KEY_VALUE_HEADS, HEAD_SIZE
    )
    attn_seq, log_totals = lax.map(attend, (query_sequence, key_sequence, value_sequence))
    attn_flat = attn_seq.reshape(token_count, QUERY_HEADS * HEAD_SIZE)
    branch = jnp.dot(attn_flat, w_out, preferred_element_type=jnp.float32)
    resid = x_float + branch
    h_two, normal_two, inverse_two = norm_forward(resid, norm_ffn)
    logits = jnp.dot(h_two, w_router, preferred_element_type=jnp.float32)
    router_probs = jax.nn.softmax(logits, -1)
    expert_ids = jnp.arange(experts_all)
    chosen = jnp.max(
        (routes[:, :, None] == jnp.arange(experts_all)[None, None, :]).astype(jnp.float32), 1
    )
    combine = chosen * router_probs
    h_all = lax.all_gather(h_two, "ep", axis=0, tiled=True)
    combine_all = lax.all_gather(combine, "ep", axis=0, tiled=True)
    holder = lax.axis_index("ep")
    held = w_gate.shape[0]
    weight = lax.dynamic_slice_in_dim(combine_all, holder * held, held, 1)
    y_part = jnp.zeros((h_all.shape[0], width), jnp.float32)
    dh_part = jnp.zeros((h_all.shape[0], width), jnp.float32)
    d_router_cols, grads = ([], [])
    gh_list, dg_list, du_list = ([], [], [])
    for e in range(held):
        gate_pre = jnp.dot(h_all, w_gate[e], preferred_element_type=jnp.float32)
        up_pre = jnp.dot(h_all, w_up[e], preferred_element_type=jnp.float32)
        back = jnp.einsum("td,fd->tf", cot_all, w_down[e], preferred_element_type=jnp.float32)
        column = weight[:, e : e + 1]
        sigma = jax.nn.sigmoid(gate_pre)
        swish = gate_pre * sigma
        hidden = (swish * up_pre).astype(jnp.bfloat16).astype(jnp.float32)
        d_router_cols.append(jnp.sum(hidden * back, -1))
        d_hidden = column * back
        dg = (d_hidden * up_pre * sigma * (1.0 + gate_pre * (1.0 - sigma))).astype(jnp.bfloat16)
        du = (d_hidden * swish).astype(jnp.bfloat16)
        gh = (column * hidden).astype(jnp.bfloat16)
        gh_list.append(gh)
        dg_list.append(dg)
        du_list.append(du)
        grads.append(
            (
                jnp.einsum("td,tf->df", h_all, dg, preferred_element_type=jnp.float32).astype(
                    jnp.bfloat16
                ),
                jnp.einsum("td,tf->df", h_all, du, preferred_element_type=jnp.float32).astype(
                    jnp.bfloat16
                ),
                jnp.einsum("tf,td->fd", gh, cot_all, preferred_element_type=jnp.float32).astype(
                    jnp.bfloat16
                ),
            )
        )
    gh_all, dg_all, du_all = (jnp.concatenate(v, 1) for v in (gh_list, dg_list, du_list))
    y_part = jnp.dot(gh_all, w_down.reshape(-1, width), preferred_element_type=jnp.float32).astype(
        jnp.bfloat16
    )
    wg_t = jnp.transpose(w_gate, (1, 0, 2)).reshape(width, -1)
    wu_t = jnp.transpose(w_up, (1, 0, 2)).reshape(width, -1)
    dh_part = (
        jnp.einsum("tf,df->td", dg_all, wg_t, preferred_element_type=jnp.float32)
        + jnp.einsum("tf,df->td", du_all, wu_t, preferred_element_type=jnp.float32)
    ).astype(jnp.bfloat16)
    d_router_held = jnp.stack(d_router_cols, 1)
    d_router_wide = lax.dynamic_update_slice_in_dim(
        jnp.zeros((h_all.shape[0], experts_all), jnp.float32), d_router_held, holder * held, 1
    )
    d_router = chosen * lax.psum_scatter(d_router_wide, "ep", scatter_dimension=0, tiled=True)
    dh_sum = lax.psum_scatter(dh_part, "ep", scatter_dimension=0, tiled=True)
    moe_sum = lax.psum_scatter(y_part, "ep", scatter_dimension=0, tiled=True)
    mixed = (resid + moe_sum.astype(jnp.float32)).astype(jnp.bfloat16)
    d_out = cotangent.astype(jnp.float32)
    d_logits = (
        router_probs * (d_router - jnp.sum(router_probs * d_router, -1, keepdims=True))
    ).astype(jnp.bfloat16)
    grad_router = jnp.einsum("td,te->de", h_two, d_logits, preferred_element_type=jnp.float32)
    d_htwo = jnp.einsum("te,de->td", d_logits, w_router, preferred_element_type=jnp.float32)
    d_htwo = d_htwo + dh_sum.astype(jnp.float32)
    grad_gate, grad_up, grad_down = (jnp.stack([g[i] for g in grads]) for i in range(3))
    d_resid_norm, grad_norm_ffn = norm_backward(d_htwo, normal_two, inverse_two, norm_ffn)
    d_resid = d_out + d_resid_norm
    d_branch = d_resid.astype(jnp.bfloat16)
    grad_out = jnp.einsum("ta,td->ad", attn_flat, d_branch, preferred_element_type=jnp.float32)
    attention_gradient = jnp.einsum(
        "td,ad->ta", d_branch, w_out, preferred_element_type=jnp.float32
    ).astype(jnp.bfloat16)
    attention_gradient = attention_gradient.reshape(
        sequence_total, SEQUENCE_TOKENS, KEY_VALUE_HEADS, query_groups, HEAD_SIZE
    )
    d_q_rot, rotated_key_gradient, value_sequence_gradient = lax.map(
        attend_back, (query_sequence, key_sequence, value_sequence, attention_gradient, log_totals)
    )
    d_q_pre = (
        invert_rotary(
            d_q_rot.reshape(token_count, QUERY_HEADS, HEAD_SIZE), cosine_table, sine_table
        )
        .reshape(token_count, QUERY_HEADS * HEAD_SIZE)
        .astype(jnp.bfloat16)
    )
    d_k_pre = (
        invert_rotary(
            rotated_key_gradient.reshape(token_count, KEY_VALUE_HEADS, HEAD_SIZE),
            cosine_table,
            sine_table,
        )
        .reshape(token_count, KEY_VALUE_HEADS * HEAD_SIZE)
        .astype(jnp.bfloat16)
    )
    value_rows_gradient = value_sequence_gradient.reshape(
        token_count, KEY_VALUE_HEADS * HEAD_SIZE
    ).astype(jnp.bfloat16)
    grad_query = jnp.einsum("td,tq->dq", hidden_first, d_q_pre, preferred_element_type=jnp.float32)
    grad_key = jnp.einsum("td,tq->dq", hidden_first, d_k_pre, preferred_element_type=jnp.float32)
    grad_value = jnp.einsum(
        "td,tq->dq", hidden_first, value_rows_gradient, preferred_element_type=jnp.float32
    )
    d_hone = jnp.einsum("tq,dq->td", d_q_pre, w_query, preferred_element_type=jnp.float32)
    d_hone = d_hone + jnp.einsum(
        "tq,dq->td", d_k_pre, key_projection, preferred_element_type=jnp.float32
    )
    d_hone = d_hone + jnp.einsum(
        "tq,dq->td", value_rows_gradient, value_projection, preferred_element_type=jnp.float32
    )
    d_x_norm, grad_norm_attn = norm_backward(d_hone, normal_one, inverse_one, norm_attn)
    d_input = d_resid + d_x_norm
    part_na, part_q, part_k, part_v, part_o, part_nf, part_r = (
        lax.psum_scatter(
            grad_norm_attn.astype(jnp.bfloat16), "ep", scatter_dimension=0, tiled=True
        ).astype(jnp.float32),
        lax.psum_scatter(
            grad_query.astype(jnp.bfloat16), "ep", scatter_dimension=0, tiled=True
        ).astype(jnp.float32),
        lax.psum_scatter(
            grad_key.astype(jnp.bfloat16), "ep", scatter_dimension=0, tiled=True
        ).astype(jnp.float32),
        lax.psum_scatter(
            grad_value.astype(jnp.bfloat16), "ep", scatter_dimension=0, tiled=True
        ).astype(jnp.float32),
        lax.psum_scatter(
            grad_out.astype(jnp.bfloat16), "ep", scatter_dimension=0, tiled=True
        ).astype(jnp.float32),
        lax.psum_scatter(
            grad_norm_ffn.astype(jnp.bfloat16), "ep", scatter_dimension=0, tiled=True
        ).astype(jnp.float32),
        lax.psum_scatter(
            grad_router.astype(jnp.bfloat16), "ep", scatter_dimension=0, tiled=True
        ).astype(jnp.float32),
    )
    part_gate, part_up, part_down = (grad_gate, grad_up, grad_down)
    sum_na, sum_q, sum_k, sum_v, sum_o, sum_nf, sum_r = lax.psum(
        (part_na, part_q, part_k, part_v, part_o, part_nf, part_r), "rep"
    )
    share_gate, share_up, share_down = (
        lax.psum_scatter(part_gate, "rep", scatter_dimension=1, tiled=True),
        lax.psum_scatter(part_up, "rep", scatter_dimension=1, tiled=True),
        lax.psum_scatter(part_down, "rep", scatter_dimension=2, tiled=True),
    )
    full_gate, full_up, full_down = (
        lax.all_gather(share_gate.astype(jnp.bfloat16), "rep", axis=1, tiled=True).astype(
            jnp.float32
        ),
        lax.all_gather(share_up.astype(jnp.bfloat16), "rep", axis=1, tiled=True).astype(
            jnp.float32
        ),
        lax.all_gather(share_down.astype(jnp.bfloat16), "rep", axis=2, tiled=True).astype(
            jnp.float32
        ),
    )
    return (
        mixed,
        d_input,
        sum_na,
        sum_q,
        sum_k,
        sum_v,
        sum_o,
        sum_nf,
        sum_r,
        full_gate,
        full_up,
        full_down,
    )


def solution(mesh):
    placed = (
        P(("rep", "ep"), None),
        P(),
        P(),
        P(),
        P(),
        P(),
        P(),
        P(),
        P("ep", None, None),
        P("ep", None, None),
        P("ep", None, None),
        P(("rep", "ep"), None),
        P(("rep", "ep"), None),
    )
    return jax.shard_map(
        per_device,
        mesh=mesh,
        in_specs=placed,
        out_specs=(
            P(("rep", "ep"), None),
            P(("rep", "ep"), None),
            P("ep"),
            P("ep", None),
            P("ep", None),
            P("ep", None),
            P("ep", None),
            P("ep"),
            P("ep", None),
            P("ep", None, None),
            P("ep", None, None),
            P("ep", None, None),
        ),
        check_vma=False,
    )
```

profile of v0, /device:TPU:0, one launch (start us, length us, event | category | flops | bytes accessed | tf_op | source)
XLA Modules:
  0.0 1600.0 jit_solution(1905756668507000208)
XLA Ops:
  18.5 10.6 fusion.9
  29.2 11.4 fusion.3
  40.7 12.0 fusion.76
  59.8 48.4 %all-gather.6.cloned.1.call-done = bf16[2048,1536]{1,0:T(8,128)(2,1)} async-done(((bf16[512,1536]{1,0:T(8,128)(2,1)}), bf16[2048,1536]{1,0:T(8,128)(2,1)}) %all-gather.6.cloned.1.call-update) | async-done | bytes 6291472 | tf_op jit(solution)/shard_map/all_gather | solution.py:151
  108.2 8.8 fusion.103
  117.0 7.6 fusion.99
  124.5 6.6 fusion.105
  131.2 5.0 fusion.101
  136.2 5.1 fusion.95
  141.3 5.1 fusion.97
  146.4 5.1 fusion.91
  151.5 5.0 fusion.93
  156.5 5.2 fusion.87
  161.7 5.0 fusion.89
  166.7 12.4 fusion.15
  179.2 10.1 fusion.17
  189.3 8.7 fusion.19
  198.0 8.9 fusion.21
  206.8 8.6 fusion.23
  217.4 10.6 copy.60
  228.0 10.6 copy.61
  240.9 5.6 all_gather.18
  246.6 9.6 constant_dynamic-update-slice_fusion.9
  259.7 6.5 constant_dynamic-update-slice_fusion.8
  267.3 7.7 constant_dynamic-update-slice_fusion.7
  275.1 8.5 constant_dynamic-update-slice_fusion.6
  284.6 8.4 constant_dynamic-update-slice_fusion.5
  293.0 21.8 %fusion.159 = f32[2048,1536]{1,0:T(8,128)} fusion(bf16[2048,2560]{0,1:T(8,128)(2,1)} %get-tuple-element.126, bf16[1536,2560]{0,1:T(8,128)(2,1)S(1)} %bitcast.298), kind=kOutput, calls=%fused_computation.266 | convolution fusion | flops 16106127360 | bytes 30932992 | tf_op jit(solution)/shard_map/tf,df->td/dot_general | solution.py:196
  314.9 21.4 %add_convert_fusion = bf16[2048,1536]{1,0:T(8,128)(2,1)} fusion(f32[2048,1536]{1,0:T(8,128)} %fusion.159, bf16[2048,2560]{0,1:T(8,128)(2,1)S(1)} %copy-done.66, bf16[1536,2560]{0,1:T(8,128)(2,1)S(1)} %bitcast.295), kind=kOutput, calls=%fused_computation.13 | convolution fusion | flops 16112418816 | bytes 37224448 | tf_op jit(solution)/shard_map/tf,df->td/dot_general | solution.py:197
  336.3 22.3 %convolution_convert_fusion.2 = bf16[2048,1536]{1,0:T(8,128)(2,1)} fusion(bf16[2048,2560]{0,1:T(8,128)(2,1)} %get-tuple-element.152, bf16[2560,1536]{1,0:T(8,128)(2,1)} %bitcast.331), kind=kOutput, calls=%fused_computation.18 | convolution fusion | flops 16109273088 | bytes 24641536 | tf_op jit(solution)/shard_map/dot_general | solution.py:190
  359.0 8.2 fusion.37
  367.2 7.6 fusion.39
  388.9 8.2 fusion.47
  397.1 7.5 fusion.49
  404.6 4.6 fusion.51
  419.1 8.2 fusion.57
  427.4 8.0 fusion.59
  449.0 15.5 copy.79
  464.6 13.7 copy.82
  481.4 5.3 multiply_reduce_fusion
  486.6 5.5 multiply_add_fusion
  493.8 6.3 convolution_convert_fusion.20
  502.0 22.2 %fusion = (f32[8,3,512]{2,1,0:T(4,128)S(1)}, f32[8,512,512,3]{2,1,3,0:T(8,128)}) fusion(f32[8,3,512]{2,1,0:T(4,128)S(1)} %log_add_fusion, f32[8,512,512,3]{2,1,3,0:T(8,128)} %get-tuple-element.160, pred[512,512]{0,1:T(8,128)(4,1)S(1)} %copy-done.10, bf16[512,8,64,1]{0,2,3,1:T(8,128)(2,1)} %bitcast.313, bf16[512,8,3,64]{0,3,2,1:T(8,128)(2,1)S(1)} %bitcast.299), kind=kOutput, calls=%fused_computation.2 | convolution fusion | flops 836751360 | bytes 52789248 | tf_op jit(solution)/shard_map/while/body/eval_jaxpr/qhgd,khd->hgqk/dot_general | solution.py:83
  524.2 23.1 %fusion.2 = bf16[8,3,512,512]{2,3,1,0:T(8,128)(2,1)} fusion(f32[8,512,512,3]{2,1,3,0:T(8,128)} %get-tuple-element.172, f32[8,3,512]{2,1,0:T(4,128)S(1)} %get-tuple-element.171, f32[8,3,512]{2,1,0:T(4,128)S(1)} %log_add_fusion, f32[8,512,512,3]{2,1,3,0:T(8,128)} %get-tuple-element.160, pred[512,512]{0,1:T(8,128)(4,1)S(1)} %copy-done.10), kind=kLoop, calls=%fused_computation.4 | loop fusion | flops 37748736 | bytes 63275008 | tf_op jit(solution)/shard_map/while/body/eval_jaxpr/convert_element_type | solution.py:85
  547.3 8.6 fusion.126
  559.6 12.2 fusion.127
  575.0 7.0 convolution_multiply_fusion
  588.5 7.3 convolution_convert_fusion
  599.9 143.3 %reduce-scatter.32.cloned.1.call-done = bf16[5,192,512]{2,1,0:T(8,128)(2,1)} async-done(((bf16[5,1536,512]{2,1,0:T(8,128)(2,1)}), bf16[5,192,512]{2,1,0:T(8,128)(2,1)}) %reduce-scatter.32.cloned.1.call-update) | async-done | bytes 983056 | tf_op jit(solution)/shard_map/reduce_scatter | solution.py:290
  743.5 142.5 %reduce-scatter.36.cloned.1.call-done = bf16[192,2560]{1,0:T(8,128)(2,1)} async-done(((bf16[1536,2560]{1,0:T(8,128)(2,1)}), bf16[192,2560]{1,0:T(8,128)(2,1)}) %reduce-scatter.36.cloned.1.call-update) | async-done | bytes 983056
  893.4 15.0 reduce-scatter.34.cloned.1.call-done
  909.4 5.2 fusion.160
  919.1 5.8 all-reduce.3
  925.1 5.3 fusion.33
  930.4 9.2 reduce-scatter.24.cloned.1.call-done
  939.6 30.9 %reduce-scatter.26.cloned.1.call-done = bf16[384,512]{1,0:T(8,128)(2,1)} async-done(((bf16[1536,512]{1,0:T(8,128)(2,1)}), bf16[384,512]{1,0:T(8,128)(2,1)}) %reduce-scatter.26.cloned.1.call-update) | async-done | bytes 393232 | tf_op jit(solution)/shard_map/reduce_scatter | solution.py:271
  970.5 50.8 %reduce-scatter.22.cloned.1.call-done = bf16[384,1536]{1,0:T(8,128)(2,1)} async-done(((bf16[1536,1536]{1,0:T(8,128)(2,1)}), bf16[384,1536]{1,0:T(8,128)(2,1)}) %reduce-scatter.22.cloned.1.call-update) | async-done | bytes 1179664 | tf_op jit(solution)/shard_map/reduce_scatter | solution.py:265
  1021.3 50.6 %reduce-scatter.28.cloned.1.call-done = bf16[384,1536]{1,0:T(8,128)(2,1)} async-done(((bf16[1536,1536]{1,0:T(8,128)(2,1)}), bf16[384,1536]{1,0:T(8,128)(2,1)}) %reduce-scatter.28.cloned.1.call-update) | async-done | bytes 1179664 | tf_op jit(solution)/shard_map/reduce_scatter | solution.py:274
  1071.9 310.1 %all-reduce.5 = (f32[384]{0:T(512)}, f32[384,1536]{1,0:T(8,128)}, f32[384,512]{1,0:T(8,128)}, f32[384,512]{1,0:T(8,128)}, f32[384,1536]{1,0:T(8,128)}, /*index=5*/f32[384]{0:T(512)}, f32[384,20]{0,1:T(8,128)}) all-reduce(f32[384]{0:T(512)S(1)} %dynamic-slice_convert_fusion.1, ...), channel_id=1, replica_groups=mesh['rep'=8,'ep'=4] {'rep'}, use_global_device_ids=true, to_apply=%region_21.22 | all-reduce | flops 1581312 | bytes 9489408 | tf_op jit(solution)/shard_map/psum | solution.py:285
  1382.0 11.2 convert_element_type.368
  1393.2 69.8 %all-gather.12.cloned.1.call-done = bf16[5,1536,512]{2,1,0:T(8,128)(2,1)} async-done(((bf16[5,192,512]{2,1,0:T(8,128)(2,1)}), bf16[5,1536,512]{2,1,0:T(8,128)(2,1)}) %all-gather.12.cloned.1.call-update) | async-done | bytes 7864336 | tf_op jit(solution)/shard_map/all_gather | solution.py:297
  1463.0 11.6 convert_element_type.374
  1474.6 107.0 %all-gather.14.cloned.1.call-done = bf16[5,512,1536]{1,2,0:T(8,128)(2,1)} async-done(((bf16[5,512,192]{1,2,0:T(8,128)(2,1)}), bf16[5,512,1536]{1,2,0:T(8,128)(2,1)}) %all-gather.14.cloned.1.call-update) | async-done | bytes 7864336 | tf_op jit(solution)/shard_map/all_gather | solution.py:300
  1581.6 11.4 copy.67
  (343 shorter events, 102.2 us)
Async XLA Ops:
  7.2 101.0 %all-gather.6.cloned.1.call-start = ((), (), s32[]{:S(2)}) async-start(), calls=%async_computation.11 | async-start | bytes 7864320 | tf_op jit(solution)/shard_map/all_gather | solution.py:151
  10.6 30.0 %copy-start.9 = (pred[512,512]{0,1:T(8,128)(4,1)}, pred[512,512]{0,1:T(8,128)(4,1)S(1)}, u32[]{:S(2)}) copy-start(pred[512,512]{0,1:T(8,128)(4,1)S(1)} %broadcast_compare_fusion) | copy-start | bytes 786436
  13.3 27.4 %copy-start.63 = (bf16[512,512]{0,1:T(8,128)(2,1)}, bf16[512,512]{0,1:T(8,128)(2,1)S(1)}, u32[]{:S(2)}) copy-start(bf16[512,512]{0,1:T(8,128)(2,1)S(1)} %convolution_convert_fusion.22) | copy-start | bytes 1572868
  17.7 11.5 copy-start.49
  17.7 11.5 copy-start.51
  18.3 10.9 copy-start.28
  18.3 10.9 copy-start.30
  18.5 10.7 copy-start.56
  18.5 10.7 copy-start.58
  29.2 11.5 copy-start.69
  29.2 23.5 %slice-start.16 = ((s8[4718592]{0:T(1024)(128)(4,1)}), s8[4194304]{0:T(1024)(128)(4,1)S(1)}, s32[]{:S(2)}) async-start(s8[4718592]{0:T(1024)(128)(4,1)} %bitcast.340), calls=%async_computation.43 | async-start | bytes 8388608
  40.6 12.1 copy-start.71
  40.7 12.1 slice-start.17
  59.0 107.7 %all-gather.8.cloned.1.call-start = ((), (), s32[]{:S(2)}) async-start(), calls=%async_computation.13 | async-start | bytes 7864320 | tf_op jit(solution)/shard_map/all_gather | solution.py:118
  59.7 179.1 %reduce-scatter.18.cloned.1.call-start = ((), (), s32[]{:S(2)}) async-start(), calls=%async_computation.14 | async-start | bytes 245760 | tf_op jit(solution)/shard_map/reduce_scatter | solution.py:203
  117.0 14.2 slice-start
  124.5 11.7 slice-start.2
  166.7 12.4 copy-start.23
  166.7 12.4 copy-start.25
  166.7 22.5 %slice-start.8 = ((s8[7864320]{0:T(1024)(128)(4,1)}), s8[4194304]{0:T(1024)(128)(4,1)S(1)}, s32[]{:S(2)}) async-start(s8[7864320]{0:T(1024)(128)(4,1)} %bitcast.332), calls=%async_computation.35 | async-start | bytes 8388608
  179.1 10.1 copy-start.19
  179.1 10.1 copy-start.21
  179.1 10.1 slice-start.9
  206.8 10.0 copy-start.2
  206.8 10.0 copy-start.67
  216.7 264.6 %reduce-scatter.20.cloned.1.call-start = ((), (), s32[]{:S(2)}) async-start(), calls=%async_computation.15 | async-start | bytes 7864320 | tf_op jit(solution)/shard_map/reduce_scatter | solution.py:204
  217.3 21.5 %copy-start.59 = (f32[512,20]{0,1:T(8,128)}, f32[512,20]{0,1:T(8,128)S(1)}, u32[]{:S(2)}) copy-start(f32[512,20]{0,1:T(8,128)S(1)} %get-tuple-element.164) | copy-start | bytes 122884
  217.4 21.5 %copy-start.78 = (f32[512]{0:T(512)}, f32[512]{0:T(512)S(1)}, u32[]{:S(2)}) copy-start(f32[512]{0:T(512)S(1)} %get-tuple-element.163) | copy-start | bytes 6148
  228.0 10.7 copy-start.96
  238.7 17.5 %copy-start.94 = (f32[512]{0:T(512)}, f32[512]{0:T(512)S(1)}, u32[]{:S(2)}) copy-start(f32[512]{0:T(512)S(1)} %fusion.134) | copy-start | bytes 6148
  246.5 9.7 copy-start.88
  246.5 9.7 copy-start.86
  246.5 19.6 %copy-start.84 = (f32[2048,1]{0,1:T(1,128)}, f32[2048,1]{0,1:T(1,128)S(1)}, u32[]{:S(2)}) copy-start(f32[2048,1]{0,1:T(1,128)S(1)} %get-tuple-element.148) | copy-start | bytes 24580
  246.5 28.5 %copy-start.82 = (f32[2048,1]{0,1:T(1,128)}, f32[2048,1]{0,1:T(1,128)S(1)}, u32[]{:S(2)}) copy-start(f32[2048,1]{0,1:T(1,128)S(1)} %get-tuple-element.147) | copy-start | bytes 24580
  246.5 37.1 %copy-start.80 = (f32[2048,1]{0,1:T(1,128)}, f32[2048,1]{0,1:T(1,128)S(1)}, u32[]{:S(2)}) copy-start(f32[2048,1]{0,1:T(1,128)S(1)} %get-tuple-element.146) | copy-start | bytes 24580
  246.6 11.3 copy-start.26
  246.6 12.5 copy-start.27
  246.6 13.1 copy-start.34
  275.1 17.9 %slice-start.6 = ((s8[7864320]{0:T(1024)(128)(4,1)}), s8[4194304]{0:T(1024)(128)(4,1)S(1)}, s32[]{:S(2)}) async-start(s8[7864320]{0:T(1024)(128)(4,1)} %bitcast.296), calls=%async_computation.33 | async-start | bytes 8388608
  284.6 30.2 %slice-start.4 = ((s8[7864320]{0:T(1024)(128)(4,1)}), s8[4194304]{0:T(1024)(128)(4,1)S(1)}, s32[]{:S(2)}) async-start(s8[7864320]{0:T(1024)(128)(4,1)} %bitcast.293), calls=%async_computation.31 | async-start | bytes 8388608
  293.0 21.9 %slice-start.5 = ((s8[7864320]{0:T(1024)(128)(4,1)}), s8[3670016]{0:T(1024)(128)(4,1)S(1)}, s32[]{:S(2)}) async-start(s8[7864320]{0:T(1024)(128)(4,1)} %bitcast.293), calls=%async_computation.32 | async-start | bytes 7340032
  293.0 21.9 %copy-start.66 = (bf16[2048,2560]{0,1:T(8,128)(2,1)S(1)}, bf16[2048,2560]{0,1:T(8,128)(2,1)}, u32[]{:S(2)}) copy-start(bf16[2048,2560]{0,1:T(8,128)(2,1)} %get-tuple-element.94) | copy-start | bytes 31457284
  336.3 150.3 %reduce-scatter.16.cloned.1.call-start = ((), (), s32[]{:S(2)}) async-start(), calls=%async_computation.12 | async-start | bytes 7864320 | tf_op jit(solution)/shard_map/reduce_scatter | solution.py:205
  358.7 241.1 %reduce-scatter.30.cloned.1.call-start = ((), (), s32[]{:S(2)}) async-start(), calls=%async_computation.20 | async-start | bytes 8847360 | tf_op jit(solution)/shard_map/reduce_scatter | solution.py:289
  358.9 15.8 slice-start.12
  388.6 354.6 %reduce-scatter.32.cloned.1.call-start = ((), (), s32[]{:S(2)}) async-start(), calls=%async_computation.22 | async-start | bytes 8847360 | tf_op jit(solution)/shard_map/reduce_scatter | solution.py:290
  388.9 15.7 slice-start.14
  418.4 467.5 %reduce-scatter.36.cloned.1.call-start = ((), (), s32[]{:S(2)}) async-start(), calls=%async_computation.26 | async-start | bytes 8847360
  419.1 16.3 %slice-start.10 = ((s8[6291456]{0:T(1024)(128)(4,1)}), s8[4194304]{0:T(1024)(128)(4,1)S(1)}, s32[]{:S(2)}) async-start(s8[6291456]{0:T(1024)(128)(4,1)} %bitcast.334), calls=%async_computation.37 | async-start | bytes 8388608
  478.3 430.1 %reduce-scatter.34.cloned.1.call-start = ((), (), s32[]{:S(2)}) async-start(), calls=%async_computation.25 | async-start | bytes 491520
  479.1 45.0 %copy-start.62 = (f32[8,3,512]{2,1,0:T(4,128)}, f32[8,3,512]{2,1,0:T(4,128)S(1)}, u32[]{:S(2)}) copy-start(f32[8,3,512]{2,1,0:T(4,128)S(1)} %log_add_fusion) | copy-start | bytes 147460
  481.1 458.5 %reduce-scatter.24.cloned.1.call-start = ((), (), s32[]{:S(2)}) async-start(), calls=%async_computation.17 | async-start | bytes 1966080 | tf_op jit(solution)/shard_map/reduce_scatter | solution.py:268
  501.9 22.2 %copy-start.7 = (bf16[512,1536]{0,1:T(8,128)(2,1)}, bf16[512,1536]{0,1:T(8,128)(2,1)S(1)}, u32[]{:S(2)}) copy-start(bf16[512,1536]{0,1:T(8,128)(2,1)S(1)} %copy.62) | copy-start | bytes 4718596
  524.2 23.1 %copy-start.29 = (bf16[512,24,32]{0,2,1:T(8,128)(2,1)S(1)}, bf16[512,24,32]{0,2,1:T(8,128)(2,1)}, u32[]{:S(2)}) copy-start(bf16[512,24,32]{0,2,1:T(8,128)(2,1)} %copy-done.28) | copy-start | bytes 2359300
  524.2 23.1 %copy-start.31 = (bf16[512,24,32]{0,2,1:T(8,128)(2,1)S(1)}, bf16[512,24,32]{0,2,1:T(8,128)(2,1)}, u32[]{:S(2)}) copy-start(bf16[512,24,32]{0,2,1:T(8,128)(2,1)} %copy-done.30) | copy-start | bytes 2359300
  547.3 9.7 copy-start.5
  547.3 9.7 copy-start.77
  559.3 411.1 %reduce-scatter.26.cloned.1.call-start = ((), (), s32[]{:S(2)}) async-start(), calls=%async_computation.18 | async-start | bytes 1966080 | tf_op jit(solution)/shard_map/reduce_scatter | solution.py:271
  574.9 446.4 %reduce-scatter.22.cloned.1.call-start = ((), (), s32[]{:S(2)}) async-start(), calls=%async_computation.16 | async-start | bytes 5898240 | tf_op jit(solution)/shard_map/reduce_scatter | solution.py:265
  588.4 483.5 %reduce-scatter.28.cloned.1.call-start = ((), (), s32[]{:S(2)}) async-start(), calls=%async_computation.19 | async-start | bytes 5898240 | tf_op jit(solution)/shard_map/reduce_scatter | solution.py:274
  595.8 296.4 %copy-start.102 = (u32[32]{0:T(128)S(1)}, u32[32]{0:T(128)}, u32[]{:S(2)}) copy-start(u32[32]{0:T(128)} %constant.122) | copy-start | bytes 388
  595.8 786.2 %all-gather.10.cloned.1.call-start = ((), (), s32[]{:S(2)}) async-start(), calls=%async_computation.21 | async-start | bytes 8847360 | tf_op jit(solution)/shard_map/all_gather | solution.py:294
  599.9 863.1 %all-gather.12.cloned.1.call-start = ((), (), s32[]{:S(2)}) async-start(), calls=%async_computation.23 | async-start | bytes 8847360 | tf_op jit(solution)/shard_map/all_gather | solution.py:297
  743.2 838.4 %all-gather.14.cloned.1.call-start = ((), (), s32[]{:S(2)}) async-start(), calls=%async_computation.24 | async-start | bytes 8847360 | tf_op jit(solution)/shard_map/all_gather | solution.py:300
  (73 other events, 383.6 us)
Sparse Core Ops, SparseCore 0:
  59.1 49.0 all-gather.5
  109.7 46.3 all-gather.7
  216.9 19.7 reduce-scatter.17
  336.4 58.3 reduce-scatter.19
  397.4 58.3 reduce-scatter.15
  459.8 139.9 reduce-scatter.29
  604.0 139.0 reduce-scatter.31
  746.8 139.0 reduce-scatter.35
  888.5 19.8 reduce-scatter.33
  911.4 28.1 reduce-scatter.23
  942.3 28.1 reduce-scatter.25
  973.4 47.8 reduce-scatter.21
  1024.0 47.8 reduce-scatter.27
  1073.9 246.2 all-gather.9
  1322.3 140.6 all-gather.11
  1465.0 116.5 all-gather.13
where the time goes:
time: 1610 us; the launch traced here: 1600 us
  waiting for transfers between devices  672 us (42%)
  matrix products  382 us (24%)
  blocking collectives  322 us (20%)
  other arithmetic  118 us (7%)
  local copies, waits for them, and re-layouts  87.7 us (5%)
  between operations  16.6 us (1%)
    psum x1, blocking collectives, per_device(): lax.psum((part_na, part_q, part_k, part_v, part_o, part_nf, part_r), 'rep')  310 us
    unnamed x18, waiting for transfers between devices  158 us
    reduce_scatter x1, waiting for transfers between devices, per_device(): lax.psum_scatter(part_up, 'rep', scatter_dimension=1, tiled=True)  143 us
    all_gather x1, waiting for transfers between devices, per_device(): lax.all_gather(share_down.astype(jnp.bfloat16), 'rep', axis=2, tiled=True)  107 us
    unnamed x251, local copies, waits for them, and re-layouts  82.6 us
    all_gather x1, waiting for transfers between devices, per_device(): lax.all_gather(share_up.astype(jnp.bfloat16), 'rep', axis=1, tiled=True)  69.8 us
    reduce_scatter x1, waiting for transfers between devices, per_device(): lax.psum_scatter(grad_query.astype(jnp.bfloat16), 'ep', scatter_dimension...  50.8 us
    reduce_scatter x1, waiting for transfers between devices, per_device(): lax.psum_scatter(grad_out.astype(jnp.bfloat16), 'ep', scatter_dimension=0...  50.6 us
  transfers between devices with their start and end apart: 16, of which 11 were waited for; matrix products, arithmetic and copies ran while one was open for 24% of the time, Pallas kernels for 0%

commit v1 on v0

--- a/solution.py
+++ b/solution.py
@@ -148,7 +148,12 @@
         (routes[:, :, None] == jnp.arange(experts_all)[None, None, :]).astype(jnp.float32), 1
     )
     combine = chosen * router_probs
-    h_all = lax.all_gather(h_two, "ep", axis=0, tiled=True)
+    ring = [h_two]
+    for hop in range(3):
+        ring.append(lax.ppermute(ring[-1], "ep", [(dev, (dev + 1) % 4) for dev in range(4)]))
+    h_all = jnp.roll(
+        jnp.concatenate(ring[::-1], axis=0), (lax.axis_index("ep") + 1) * ring[0].shape[0], axis=0
+    )
     combine_all = lax.all_gather(combine, "ep", axis=0, tiled=True)
     holder = lax.axis_index("ep")
     held = w_gate.shape[0]

time: 1610 us -> 1670 us (1.037)
  matrix products: 382 us -> 421 us
    ppermute x0 -> x3, waiting for transfers between devices: none -> 72.9 us  [per_device(): lax.ppermute(ring[-1], 'ep', [(dev, (dev + 1) % 4) for dev in range(4)])]
    all_gather x1 -> x0, waiting for transfers between devices: 48.4 us -> none  [per_device(): h_all = lax.all_gather(h_two, 'ep', axis=0, tiled=True)]
    unnamed x251 -> x249, local copies, waits for them, and re-layouts: 82.6 us -> 96.3 us
    unnamed x13 -> x12, other arithmetic: 32.3 us -> 34 us
    unnamed x18 -> x17, waiting for transfers between devices: 158 us -> 158 us
  transfers between devices with their start and end apart: 16 -> 18, of which waited for: 11 -> 13; matrix products, arithmetic and copies ran while one was open for 24% -> 26% of each run, Pallas kernels for 0% -> 0%
where the time goes in v1:
time: 1670 us
  waiting for transfers between devices  684 us (41%)
  matrix products  421 us (25%)
  blocking collectives  322 us (19%)
  other arithmetic  120 us (7%)
  local copies, waits for them, and re-layouts  101 us (6%)
    psum x1, blocking collectives, per_device(): lax.psum((part_na, part_q, part_k, part_v, part_o, part_nf, part_r), 'rep')  310 us
    unnamed x17, waiting for transfers between devices  158 us
    reduce_scatter x1, waiting for transfers between devices, per_device(): lax.psum_scatter(part_up, 'rep', scatter_dimension=1, tiled=True)  130 us
    all_gather x1, waiting for transfers between devices, per_device(): lax.all_gather(share_down.astype(jnp.bfloat16), 'rep', axis=2, tiled=True)  107 us
    unnamed x249, local copies, waits for them, and re-layouts  96.3 us
    ppermute x3, waiting for transfers between devices, per_device(): lax.ppermute(ring[-1], 'ep', [(dev, (dev + 1) % 4) for dev in range(4)])  72.9 us
    all_gather x1, waiting for transfers between devices, per_device(): lax.all_gather(share_up.astype(jnp.bfloat16), 'rep', axis=1, tiled=True)  69.8 us
    reduce_scatter x1, waiting for transfers between devices, per_device(): lax.psum_scatter(grad_query.astype(jnp.bfloat16), 'ep', scatter_dimension...  51 us
  transfers between devices with their start and end apart: 18, of which 13 were waited for; matrix products, arithmetic and copies ran while one was open for 26% of the time, Pallas kernels for 0%

profile of v1, /device:TPU:0, one launch (start us, length us, event | category | flops | bytes accessed | tf_op | source)
XLA Modules:
  0.0 1667.4 jit_solution(7396880490317044528)
XLA Ops:
  18.5 10.9 fusion.9
  29.5 11.4 fusion.3
  40.9 12.0 fusion.76
  59.7 20.0 %collective-permute-done = bf16[512,1536]{1,0:T(8,128)(2,1)S(1)} collective-permute-done((bf16[512,1536]{1,0:T(8,128)(2,1)S(1)}, bf16[512,1536]{1,0:T(8,128)(2,1)S(1)}, u32[]{:S(2)}, u32[]{:S(2)}) %collective-permute-start) | collective-permute-done | bytes 1572896 | tf_op jit(solution)/shard_map/ppermute | solution.py:153
  79.7 19.9 %collective-permute-done.1 = bf16[512,1536]{1,0:T(8,128)(2,1)} collective-permute-done((bf16[512,1536]{1,0:T(8,128)(2,1)S(1)}, bf16[512,1536]{1,0:T(8,128)(2,1)}, u32[]{:S(2)}, u32[]{:S(2)}) %collective-permute-start.1) | collective-permute-done | bytes 1572896 | tf_op jit(solution)/shard_map/ppermute | solution.py:153
  99.7 32.9 %collective-permute-done.2 = bf16[512,1536]{1,0:T(8,128)(2,1)} collective-permute-done((bf16[512,1536]{1,0:T(8,128)(2,1)}, bf16[512,1536]{1,0:T(8,128)(2,1)}, u32[]{:S(2)}, u32[]{:S(2)}) %collective-permute-start.2) | collective-permute-done | bytes 1572896 | tf_op jit(solution)/shard_map/ppermute | solution.py:153
  149.4 8.5 fusion.103
  157.8 7.8 fusion.99
  165.6 7.8 fusion.105
  173.4 7.8 fusion.101
  181.2 7.8 fusion.95
  189.0 7.8 fusion.97
  196.8 7.8 fusion.91
  204.6 8.0 fusion.93
  212.6 7.8 fusion.87
  220.4 7.8 fusion.89
  228.2 12.3 fusion.15
  240.6 10.1 fusion.17
  250.7 9.1 fusion.19
  259.9 8.7 fusion.21
  268.6 8.6 fusion.23
  279.1 10.6 copy.60
  289.7 10.7 copy.61
  312.9 9.8 constant_dynamic-update-slice_fusion.17
  326.0 6.5 constant_dynamic-update-slice_fusion.16
  333.7 7.8 constant_dynamic-update-slice_fusion.15
  341.5 8.5 constant_dynamic-update-slice_fusion.14
  351.0 8.4 constant_dynamic-update-slice_fusion.13
  359.4 21.5 %fusion.159 = f32[2048,1536]{1,0:T(8,128)} fusion(bf16[2048,2560]{0,1:T(8,128)(2,1)} %get-tuple-element.126, bf16[1536,2560]{0,1:T(8,128)(2,1)S(1)} %bitcast.278), kind=kOutput, calls=%fused_computation.275 | convolution fusion | flops 16106127360 | bytes 30932992 | tf_op jit(solution)/shard_map/tf,df->td/dot_general | solution.py:201
  380.9 21.4 %add_convert_fusion = bf16[2048,1536]{1,0:T(8,128)(2,1)} fusion(f32[2048,1536]{1,0:T(8,128)} %fusion.159, bf16[2048,2560]{0,1:T(8,128)(2,1)S(1)} %copy-done.68, bf16[1536,2560]{0,1:T(8,128)(2,1)S(1)} %bitcast.275), kind=kOutput, calls=%fused_computation.13 | convolution fusion | flops 16112418816 | bytes 37224448 | tf_op jit(solution)/shard_map/tf,df->td/dot_general | solution.py:202
  402.4 22.3 %convolution_convert_fusion.2 = bf16[2048,1536]{1,0:T(8,128)(2,1)} fusion(bf16[2048,2560]{0,1:T(8,128)(2,1)} %get-tuple-element.152, bf16[2560,1536]{1,0:T(8,128)(2,1)} %bitcast.311), kind=kOutput, calls=%fused_computation.18 | convolution fusion | flops 16109273088 | bytes 24641536 | tf_op jit(solution)/shard_map/dot_general | solution.py:195
  425.2 8.6 fusion.37
  433.8 7.5 fusion.39
  441.3 7.5 fusion.41
  448.8 7.5 fusion.43
  456.3 7.4 fusion.45
  464.0 8.2 fusion.47
  472.2 9.1 fusion.49
  481.2 7.5 fusion.51
  488.8 7.5 fusion.53
  496.3 7.5 fusion.55
  504.5 8.3 fusion.57
  512.8 7.8 fusion.59
  534.2 15.7 copy.79
  549.9 13.1 copy.82
  586.8 22.2 %fusion = (f32[8,3,512]{2,1,0:T(4,128)S(1)}, f32[8,512,512,3]{2,1,3,0:T(8,128)}) fusion(f32[8,3,512]{2,1,0:T(4,128)S(1)} %log_add_fusion, f32[8,512,512,3]{2,1,3,0:T(8,128)} %get-tuple-element.160, pred[512,512]{0,1:T(8,128)(4,1)S(1)} %copy-done.12, bf16[512,8,64,1]{0,2,3,1:T(8,128)(2,1)} %bitcast.293, bf16[512,8,3,64]{0,3,2,1:T(8,128)(2,1)S(1)} %bitcast.279), kind=kOutput, calls=%fused_computation.2 | convolution fusion | flops 836751360 | bytes 52789248 | tf_op jit(solution)/shard_map/while/body/eval_jaxpr/qhgd,khd->hgqk/dot_general | solution.py:83
  609.0 22.7 %fusion.2 = bf16[8,3,512,512]{2,3,1,0:T(8,128)(2,1)} fusion(f32[8,512,512,3]{2,1,3,0:T(8,128)} %get-tuple-element.172, f32[8,3,512]{2,1,0:T(4,128)S(1)} %get-tuple-element.171, f32[8,3,512]{2,1,0:T(4,128)S(1)} %log_add_fusion, f32[8,512,512,3]{2,1,3,0:T(8,128)} %get-tuple-element.160, pred[512,512]{0,1:T(8,128)(4,1)S(1)} %copy-done.12), kind=kLoop, calls=%fused_computation.4 | loop fusion | flops 37748736 | bytes 63275008 | tf_op jit(solution)/shard_map/while/body/eval_jaxpr/convert_element_type | solution.py:85
  631.8 8.7 fusion.126
  644.1 11.7 fusion.127
  659.1 7.0 convolution_multiply_fusion
  672.6 7.2 convolution_convert_fusion
  680.6 130.1 %reduce-scatter.32.cloned.1.call-done = bf16[5,192,512]{2,1,0:T(8,128)(2,1)} async-done(((bf16[5,1536,512]{2,1,0:T(8,128)(2,1)}), bf16[5,192,512]{2,1,0:T(8,128)(2,1)}) %reduce-scatter.32.cloned.1.call-update) | async-done | bytes 983056 | tf_op jit(solution)/shard_map/reduce_scatter | solution.py:295
  811.0 142.5 %reduce-scatter.36.cloned.1.call-done = bf16[192,2560]{1,0:T(8,128)(2,1)} async-done(((bf16[1536,2560]{1,0:T(8,128)(2,1)}), bf16[192,2560]{1,0:T(8,128)(2,1)}) %reduce-scatter.36.cloned.1.call-update) | async-done | bytes 983056
  961.0 14.9 reduce-scatter.34.cloned.1.call-done
  997.9 9.3 reduce-scatter.24.cloned.1.call-done
  1007.2 30.7 %reduce-scatter.26.cloned.1.call-done = bf16[384,512]{1,0:T(8,128)(2,1)} async-done(((bf16[1536,512]{1,0:T(8,128)(2,1)}), bf16[384,512]{1,0:T(8,128)(2,1)}) %reduce-scatter.26.cloned.1.call-update) | async-done | bytes 393232 | tf_op jit(solution)/shard_map/reduce_scatter | solution.py:276
  1038.0 51.0 %reduce-scatter.22.cloned.1.call-done = bf16[384,1536]{1,0:T(8,128)(2,1)} async-done(((bf16[1536,1536]{1,0:T(8,128)(2,1)}), bf16[384,1536]{1,0:T(8,128)(2,1)}) %reduce-scatter.22.cloned.1.call-update) | async-done | bytes 1179664 | tf_op jit(solution)/shard_map/reduce_scatter | solution.py:270
  1089.0 50.4 %reduce-scatter.28.cloned.1.call-done = bf16[384,1536]{1,0:T(8,128)(2,1)} async-done(((bf16[1536,1536]{1,0:T(8,128)(2,1)}), bf16[384,1536]{1,0:T(8,128)(2,1)}) %reduce-scatter.28.cloned.1.call-update) | async-done | bytes 1179664 | tf_op jit(solution)/shard_map/reduce_scatter | solution.py:279
  1139.4 310.1 %all-reduce.5 = (f32[384]{0:T(512)}, f32[384,1536]{1,0:T(8,128)}, f32[384,512]{1,0:T(8,128)}, f32[384,512]{1,0:T(8,128)}, f32[384,1536]{1,0:T(8,128)}, /*index=5*/f32[384]{0:T(512)}, f32[384,20]{0,1:T(8,128)}) all-reduce(f32[384]{0:T(512)S(1)} %dynamic-slice_convert_fusion.1, ...), channel_id=1, replica_groups=mesh['rep'=8,'ep'=4] {'rep'}, use_global_device_ids=true, to_apply=%region_21.22 | all-reduce | flops 1581312 | bytes 9489408 | tf_op jit(solution)/shard_map/psum | solution.py:290
  1449.4 11.2 convert_element_type.368
  1460.7 69.8 %all-gather.9.cloned.1.call-done = bf16[5,1536,512]{2,1,0:T(8,128)(2,1)} async-done(((bf16[5,192,512]{2,1,0:T(8,128)(2,1)}), bf16[5,1536,512]{2,1,0:T(8,128)(2,1)}) %all-gather.9.cloned.1.call-update) | async-done | bytes 7864336 | tf_op jit(solution)/shard_map/all_gather | solution.py:302
  1530.5 11.6 convert_element_type.374
  1542.2 107.0 %all-gather.11.cloned.1.call-done = bf16[5,512,1536]{1,2,0:T(8,128)(2,1)} async-done(((bf16[5,512,192]{1,2,0:T(8,128)(2,1)}), bf16[5,512,1536]{1,2,0:T(8,128)(2,1)}) %all-gather.11.cloned.1.call-update) | async-done | bytes 7864336 | tf_op jit(solution)/shard_map/all_gather | solution.py:305
  1649.2 11.4 copy.67
  (344 shorter events, 136.0 us)
Async XLA Ops:
  7.2 221.0 %all-gather.5.cloned.1.call-start = ((), (), s32[]{:S(2)}) async-start(), calls=%async_computation.12 | async-start | bytes 7864320 | tf_op jit(solution)/shard_map/all_gather | solution.py:118
  10.6 30.3 %copy-start.11 = (pred[512,512]{0,1:T(8,128)(4,1)}, pred[512,512]{0,1:T(8,128)(4,1)S(1)}, u32[]{:S(2)}) copy-start(pred[512,512]{0,1:T(8,128)(4,1)S(1)} %broadcast_compare_fusion) | copy-start | bytes 786436
  13.3 27.6 %copy-start.65 = (bf16[512,512]{0,1:T(8,128)(2,1)}, bf16[512,512]{0,1:T(8,128)(2,1)S(1)}, u32[]{:S(2)}) copy-start(bf16[512,512]{0,1:T(8,128)(2,1)S(1)} %convolution_convert_fusion.22) | copy-start | bytes 1572868
  17.7 11.7 copy-start.51
  17.7 11.7 copy-start.53
  18.3 11.2 copy-start.30
  18.3 11.1 copy-start.32
  18.5 11.0 copy-start.58
  18.5 11.0 copy-start.60
  29.4 11.5 copy-start.73
  29.5 23.5 %slice-start.12 = ((s8[4718592]{0:T(1024)(128)(4,1)}), s8[4194304]{0:T(1024)(128)(4,1)S(1)}, s32[]{:S(2)}) async-start(s8[4718592]{0:T(1024)(128)(4,1)} %bitcast.316), calls=%async_computation.38 | async-start | bytes 8388608
  40.9 12.1 copy-start.75
  40.9 12.1 slice-start.13
  56.1 91.8 %copy-start.79 = (f32[512]{0:T(512)}, f32[512]{0:T(512)S(1)}, u32[]{:S(2)}) copy-start(f32[512]{0:T(512)S(1)} %add_rsqrt_fusion) | copy-start | bytes 6148
  56.1 91.8 %copy-start.69 = (f32[1536]{0:T(1024)}, f32[1536]{0:T(1024)S(1)}, u32[]{:S(2)}) copy-start(f32[1536]{0:T(1024)S(1)} %convert_element_type.306) | copy-start | bytes 18436
  59.2 20.5 %collective-permute-start = (bf16[512,1536]{1,0:T(8,128)(2,1)S(1)}, bf16[512,1536]{1,0:T(8,128)(2,1)S(1)}, u32[]{:S(2)}, u32[]{:S(2)}) collective-permute-start(bf16[512,1536]{1,0:T(8,128)(2,1)S(1)} %multiply_convert_fusion.15), channel_id=1, source_target_pairs={{0,1},{1,2},{2,3},{3,0},{4,5},{5,6},{6,7},{7,4},{8,9},{9,10},{10,1... | collective-permute-start | bytes 4718600 | tf_op jit(solution)/shard_map/ppermute | solution.py:153
  79.7 19.9 %collective-permute-start.1 = (bf16[512,1536]{1,0:T(8,128)(2,1)S(1)}, bf16[512,1536]{1,0:T(8,128)(2,1)}, u32[]{:S(2)}, u32[]{:S(2)}) collective-permute-start(bf16[512,1536]{1,0:T(8,128)(2,1)S(1)} %collective-permute-done), channel_id=1, source_target_pairs={{0,1},{1,2},{2,3},{3,0},{4,5},{5,6},{6,7},{7,4},{8,9},{9,10},{10,1... | collective-permute-start | bytes 4718600 | tf_op jit(solution)/shard_map/ppermute | solution.py:153
  99.6 33.0 %collective-permute-start.2 = (bf16[512,1536]{1,0:T(8,128)(2,1)}, bf16[512,1536]{1,0:T(8,128)(2,1)}, u32[]{:S(2)}, u32[]{:S(2)}) collective-permute-start(bf16[512,1536]{1,0:T(8,128)(2,1)} %collective-permute-done.1), channel_id=1, source_target_pairs={{0,1},{1,2},{2,3},{3,0},{4,5},{5,6},{6,7},{7,4},{8,9},{9,10},{10,1... | collective-permute-start | bytes 4718600 | tf_op jit(solution)/shard_map/ppermute | solution.py:153
  99.7 204.9 %reduce-scatter.18.cloned.1.call-start = ((), (), s32[]{:S(2)}) async-start(), calls=%async_computation.13 | async-start | bytes 245760 | tf_op jit(solution)/shard_map/reduce_scatter | solution.py:208
  99.7 39.5 %copy-start.2 = (f32[512,1536]{1,0:T(8,128)S(1)}, f32[512,1536]{1,0:T(8,128)}, u32[]{:S(2)}) copy-start(f32[512,1536]{1,0:T(8,128)} %copy-done.1) | copy-start | bytes 9437188
  139.3 10.1 slice-start.2
  147.9 17.8 %slice-start = ((s8[7864320]{0:T(1024)(128)(4,1)}), s8[4194304]{0:T(1024)(128)(4,1)S(1)}, s32[]{:S(2)}) async-start(s8[7864320]{0:T(1024)(128)(4,1)} %bitcast.269), calls=%async_computation.26 | async-start | bytes 8388608
  149.3 16.3 slice-start.1
  228.2 12.4 copy-start.25
  228.2 12.4 copy-start.27
  228.2 22.5 %slice-start.8 = ((s8[7864320]{0:T(1024)(128)(4,1)}), s8[4194304]{0:T(1024)(128)(4,1)S(1)}, s32[]{:S(2)}) async-start(s8[7864320]{0:T(1024)(128)(4,1)} %bitcast.312), calls=%async_computation.34 | async-start | bytes 8388608
  240.6 10.1 copy-start.21
  240.6 10.1 copy-start.23
  240.6 10.1 slice-start.9
  268.6 10.0 copy-start.4
  268.6 10.0 copy-start.71
  278.5 288.1 %reduce-scatter.20.cloned.1.call-start = ((), (), s32[]{:S(2)}) async-start(), calls=%async_computation.14 | async-start | bytes 7864320 | tf_op jit(solution)/shard_map/reduce_scatter | solution.py:209
  279.1 25.5 %copy-start.61 = (f32[512,20]{0,1:T(8,128)}, f32[512,20]{0,1:T(8,128)S(1)}, u32[]{:S(2)}) copy-start(f32[512,20]{0,1:T(8,128)S(1)} %get-tuple-element.164) | copy-start | bytes 122884
  279.1 25.5 %copy-start.81 = (f32[512]{0:T(512)}, f32[512]{0:T(512)S(1)}, u32[]{:S(2)}) copy-start(f32[512]{0:T(512)S(1)} %get-tuple-element.163) | copy-start | bytes 6148
  289.7 10.7 copy-start.97
  300.5 22.2 %copy-start.95 = (f32[512]{0:T(512)}, f32[512]{0:T(512)S(1)}, u32[]{:S(2)}) copy-start(f32[512]{0:T(512)S(1)} %fusion.134) | copy-start | bytes 6148
  312.8 19.6 %copy-start.87 = (f32[2048,1]{0,1:T(1,128)}, f32[2048,1]{0,1:T(1,128)S(1)}, u32[]{:S(2)}) copy-start(f32[2048,1]{0,1:T(1,128)S(1)} %get-tuple-element.148) | copy-start | bytes 24580
  312.8 28.6 %copy-start.85 = (f32[2048,1]{0,1:T(1,128)}, f32[2048,1]{0,1:T(1,128)S(1)}, u32[]{:S(2)}) copy-start(f32[2048,1]{0,1:T(1,128)S(1)} %get-tuple-element.147) | copy-start | bytes 24580
  312.9 37.1 %copy-start.83 = (f32[2048,1]{0,1:T(1,128)}, f32[2048,1]{0,1:T(1,128)S(1)}, u32[]{:S(2)}) copy-start(f32[2048,1]{0,1:T(1,128)S(1)} %get-tuple-element.146) | copy-start | bytes 24580
  312.9 11.3 copy-start.28
  312.9 12.5 copy-start.29
  312.9 13.1 copy-start.36
  341.5 17.9 %slice-start.6 = ((s8[7864320]{0:T(1024)(128)(4,1)}), s8[4194304]{0:T(1024)(128)(4,1)S(1)}, s32[]{:S(2)}) async-start(s8[7864320]{0:T(1024)(128)(4,1)} %bitcast.276), calls=%async_computation.32 | async-start | bytes 8388608
  351.0 29.9 %slice-start.4 = ((s8[7864320]{0:T(1024)(128)(4,1)}), s8[4194304]{0:T(1024)(128)(4,1)S(1)}, s32[]{:S(2)}) async-start(s8[7864320]{0:T(1024)(128)(4,1)} %bitcast.273), calls=%async_computation.30 | async-start | bytes 8388608
  359.4 21.5 %slice-start.5 = ((s8[7864320]{0:T(1024)(128)(4,1)}), s8[3670016]{0:T(1024)(128)(4,1)S(1)}, s32[]{:S(2)}) async-start(s8[7864320]{0:T(1024)(128)(4,1)} %bitcast.273), calls=%async_computation.31 | async-start | bytes 7340032
  359.4 21.5 %copy-start.68 = (bf16[2048,2560]{0,1:T(8,128)(2,1)S(1)}, bf16[2048,2560]{0,1:T(8,128)(2,1)}, u32[]{:S(2)}) copy-start(bf16[2048,2560]{0,1:T(8,128)(2,1)} %get-tuple-element.94) | copy-start | bytes 31457284
  402.3 169.5 %reduce-scatter.16.cloned.1.call-start = ((), (), s32[]{:S(2)}) async-start(), calls=%async_computation.11 | async-start | bytes 7864320 | tf_op jit(solution)/shard_map/reduce_scatter | solution.py:210
  424.7 255.1 %reduce-scatter.30.cloned.1.call-start = ((), (), s32[]{:S(2)}) async-start(), calls=%async_computation.19 | async-start | bytes 8847360 | tf_op jit(solution)/shard_map/reduce_scatter | solution.py:294
  463.7 347.0 %reduce-scatter.32.cloned.1.call-start = ((), (), s32[]{:S(2)}) async-start(), calls=%async_computation.21 | async-start | bytes 8847360 | tf_op jit(solution)/shard_map/reduce_scatter | solution.py:295
  503.8 449.6 %reduce-scatter.36.cloned.1.call-start = ((), (), s32[]{:S(2)}) async-start(), calls=%async_computation.25 | async-start | bytes 8847360
  504.5 16.1 slice-start.10
  563.0 412.9 %reduce-scatter.34.cloned.1.call-start = ((), (), s32[]{:S(2)}) async-start(), calls=%async_computation.24 | async-start | bytes 491520
  563.8 45.1 %copy-start.64 = (f32[8,3,512]{2,1,0:T(4,128)}, f32[8,3,512]{2,1,0:T(4,128)S(1)}, u32[]{:S(2)}) copy-start(f32[8,3,512]{2,1,0:T(4,128)S(1)} %log_add_fusion) | copy-start | bytes 147460
  566.1 441.2 %reduce-scatter.24.cloned.1.call-start = ((), (), s32[]{:S(2)}) async-start(), calls=%async_computation.16 | async-start | bytes 1966080 | tf_op jit(solution)/shard_map/reduce_scatter | solution.py:273
  586.8 22.2 %copy-start.9 = (bf16[512,1536]{0,1:T(8,128)(2,1)}, bf16[512,1536]{0,1:T(8,128)(2,1)S(1)}, u32[]{:S(2)}) copy-start(bf16[512,1536]{0,1:T(8,128)(2,1)S(1)} %copy.62) | copy-start | bytes 4718596
  609.0 22.8 %copy-start.31 = (bf16[512,24,32]{0,2,1:T(8,128)(2,1)S(1)}, bf16[512,24,32]{0,2,1:T(8,128)(2,1)}, u32[]{:S(2)}) copy-start(bf16[512,24,32]{0,2,1:T(8,128)(2,1)} %copy-done.30) | copy-start | bytes 2359300
  609.0 22.8 %copy-start.33 = (bf16[512,24,32]{0,2,1:T(8,128)(2,1)S(1)}, bf16[512,24,32]{0,2,1:T(8,128)(2,1)}, u32[]{:S(2)}) copy-start(bf16[512,24,32]{0,2,1:T(8,128)(2,1)} %copy-done.32) | copy-start | bytes 2359300
  643.9 394.1 %reduce-scatter.26.cloned.1.call-start = ((), (), s32[]{:S(2)}) async-start(), calls=%async_computation.17 | async-start | bytes 1966080 | tf_op jit(solution)/shard_map/reduce_scatter | solution.py:276
  659.0 430.0 %reduce-scatter.22.cloned.1.call-start = ((), (), s32[]{:S(2)}) async-start(), calls=%async_computation.15 | async-start | bytes 5898240 | tf_op jit(solution)/shard_map/reduce_scatter | solution.py:270
  672.5 466.9 %reduce-scatter.28.cloned.1.call-start = ((), (), s32[]{:S(2)}) async-start(), calls=%async_computation.18 | async-start | bytes 5898240 | tf_op jit(solution)/shard_map/reduce_scatter | solution.py:279
  679.8 280.0 %copy-start.102 = (u32[32]{0:T(128)S(1)}, u32[32]{0:T(128)}, u32[]{:S(2)}) copy-start(u32[32]{0:T(128)} %constant.144) | copy-start | bytes 388
  679.8 769.6 %all-gather.7.cloned.1.call-start = ((), (), s32[]{:S(2)}) async-start(), calls=%async_computation.20 | async-start | bytes 8847360 | tf_op jit(solution)/shard_map/all_gather | solution.py:299
  680.6 850.0 %all-gather.9.cloned.1.call-start = ((), (), s32[]{:S(2)}) async-start(), calls=%async_computation.22 | async-start | bytes 8847360 | tf_op jit(solution)/shard_map/all_gather | solution.py:302
  810.7 838.5 %all-gather.11.cloned.1.call-start = ((), (), s32[]{:S(2)}) async-start(), calls=%async_computation.23 | async-start | bytes 8847360 | tf_op jit(solution)/shard_map/all_gather | solution.py:305
  (71 other events, 405.4 us)
Sparse Core Ops, SparseCore 0:
  99.8 55.2 all-gather.4
  278.6 25.9 reduce-scatter.17
  402.4 60.0 reduce-scatter.19
  465.1 58.3 reduce-scatter.15
  527.5 139.9 reduce-scatter.29
  671.6 139.0 reduce-scatter.31
  814.3 139.0 reduce-scatter.35
  955.9 19.8 reduce-scatter.33
  979.0 28.1 reduce-scatter.23
  1009.8 28.1 reduce-scatter.25
  1041.1 47.8 reduce-scatter.21
  1091.5 47.8 reduce-scatter.27
  1141.6 246.0 all-gather.6
  1389.7 140.7 all-gather.8
  1532.6 116.5 all-gather.10
